TPU v7x, 32 devices: a whole 2x2x4 slice. The times are simulated.
32 devices in a mesh: row: 4 (over x, core), col: 8 (over z, y).
Axes of the slice: x: 2, y: 2, z: 4, core: 2. Of those that a mesh axis runs over, the one named last changes fastest.
Arguments:
- video: float32 [1, 128, 64, 64, 256], P(None, 'row', 'col'), may hold values from -6 to 6
- decay_rates: float32 [3, 256, 64], replicated, may hold values from 0.5 to 4
- frequencies: float32 [3, 256, 64], replicated, may hold values from 0 to 64
- input_vec: float32 [3, 2, 256, 64], replicated, may hold values from -6 to 6
- output_vec: float32 [3, 2, 256, 64], replicated, may hold values from -3 to 3
- lowrank_vec: float32 [3, 2, 256, 64], replicated, may hold values from -3 to 3
- step_scale: float32 [3, 256], replicated, may hold values from 0.5 to 8
- skip_gain: float32 [256], replicated, may hold values from -4 to 4
Outputs:
- layer_out: float32 [1, 128, 64, 64, 256], P(None, 'row', 'col')
All inputs are finite; a program needn't handle non-finite values.
Results may differ from a plain program's by a relative error of at most 0.000076.
Values sent between devices are 32-bit elements; how exact they have to be, the bound alone decides.
No kernel may reach another device: no remote copies, remote signals or barrier semaphores. Data moves between devices by JAX's collectives and lax.ppermute only.
A program may use at most 192 MiB of HBM per device.

v0:
```python
import math

import jax
import jax.numpy as jnp
from jax import lax
from jax.sharding import PartitionSpec as P

full_precision = lax.Precision.HIGHEST


def angle_table(first_idx, second_idx, length):
    product = first_idx[:, None] * second_idx[None, :] % length
    return 2.0 * math.pi / length * product.astype(jnp.float32)


def complex_mul(left_re, left_im, right_re, right_im):
    return (left_re * right_re - left_im * right_im, left_re * right_im + left_im * right_re)


def complex_div(left_re, left_im, right_re, right_im):
    magnitude = right_re * right_re + right_im * right_im
    return (
        (left_re * right_re + left_im * right_im) / magnitude,
        (left_im * right_re - left_re * right_im) / magnitude,
    )


def cauchy_sum(num_re, num_im, inv_re, inv_im):
    real_part = jnp.einsum("cn,cln->cl", num_re, inv_re, precision=full_precision) - jnp.einsum(
        "cn,cln->cl", num_im, inv_im, precision=full_precision
    )
    imag_part = jnp.einsum("cn,cln->cl", num_re, inv_im, precision=full_precision) + jnp.einsum(
        "cn,cln->cl", num_im, inv_re, precision=full_precision
    )
    return (real_part, imag_part)


def axis_kernel(decay, oscill, input_part, output_part, lowrank_part, scales, length):
    step_size = scales / length
    two_over = (2.0 / step_size)[:, None, None]
    index = jnp.arange(length, dtype=jnp.int32)
    angles = 2.0 * math.pi / length * index.astype(jnp.float32)
    cosine = jnp.cos(angles)
    sine_vals = jnp.sin(angles)
    minus_cos = (1.0 - cosine)[None, :, None]
    plus_cos = (1.0 + cosine)[None, :, None]
    sine_col = sine_vals[None, :, None]
    den_re = two_over * minus_cos + decay[:, None, :] * plus_cos - oscill[:, None, :] * sine_col
    den_im = two_over * sine_col - decay[:, None, :] * sine_col - oscill[:, None, :] * plus_cos
    magnitude = den_re * den_re + den_im * den_im
    inv_re = den_re / magnitude
    inv_im = -den_im / magnitude
    prod_cb = complex_mul(output_part[0], output_part[1], input_part[0], input_part[1])
    prod_cp = complex_mul(output_part[0], output_part[1], lowrank_part[0], lowrank_part[1])
    prod_pb = complex_mul(lowrank_part[0], -lowrank_part[1], input_part[0], input_part[1])
    prod_pp = lowrank_part[0] * lowrank_part[0] + lowrank_part[1] * lowrank_part[1]
    cauchy_cb = cauchy_sum(prod_cb[0], prod_cb[1], inv_re, inv_im)
    cauchy_cp = cauchy_sum(prod_cp[0], prod_cp[1], inv_re, inv_im)
    cauchy_pb = cauchy_sum(prod_pb[0], prod_pb[1], inv_re, inv_im)
    cauchy_pp = cauchy_sum(prod_pp, jnp.zeros_like(prod_pp), inv_re, inv_im)
    shift_re = (1.0 + cosine)[None, :]
    shift_im = (-sine_vals)[None, :]
    cross_re, cross_im = complex_mul(cauchy_cp[0], cauchy_cp[1], cauchy_pb[0], cauchy_pb[1])
    cross_re, cross_im = complex_mul(shift_re, shift_im, cross_re, cross_im)
    lower_re, lower_im = complex_mul(shift_re, shift_im, cauchy_pp[0], cauchy_pp[1])
    quot_re, quot_im = complex_div(cross_re, cross_im, 1.0 + lower_re, lower_im)
    gen_re = 2.0 * (cauchy_cb[0] - quot_re)
    gen_im = 2.0 * (cauchy_cb[1] - quot_im)
    table = angle_table(index, index, length)
    kernel = jnp.dot(gen_re, jnp.cos(table), precision=full_precision) - jnp.dot(
        gen_im, jnp.sin(table), precision=full_precision
    )
    return (kernel / length).T


def sliced_kernels(
    decay_rates,
    frequencies,
    input_vec,
    output_vec,
    lowrank_vec,
    step_scale,
    first_chan,
    share_count,
    lengths,
):
    pieces = []
    for axis_num in range(3):
        pieces.append(
            axis_kernel(
                lax.dynamic_slice_in_dim(decay_rates[axis_num], first_chan, share_count, 0),
                lax.dynamic_slice_in_dim(frequencies[axis_num], first_chan, share_count, 0),
                lax.dynamic_slice_in_dim(input_vec[axis_num], first_chan, share_count, 1),
                lax.dynamic_slice_in_dim(output_vec[axis_num], first_chan, share_count, 1),
                lax.dynamic_slice_in_dim(lowrank_vec[axis_num], first_chan, share_count, 1),
                lax.dynamic_slice_in_dim(step_scale[axis_num], first_chan, share_count, 0),
                lengths[axis_num],
            )
        )
    return pieces


def circulant(kernel, length, causal):
    steps_idx = jnp.arange(length, dtype=jnp.int32)
    offset = steps_idx[:, None] - steps_idx[None, :]
    if causal:
        table = kernel.T[:, jnp.clip(offset, 0, length - 1)]
        return jnp.where((offset >= 0)[None], table, 0.0)
    return kernel.T[:, offset % length]


def on_device(
    video, decay_rates, frequencies, input_vec, output_vec, lowrank_vec, step_scale, skip_gain
):
    clip_count, frame_rows, height_rows, width_cells, channels = video.shape
    row_count = lax.axis_size("row")
    col_count = lax.axis_size("col")
    frames = frame_rows * row_count
    height = height_rows * col_count
    lengths = (frames, height, width_cells)
    dev_count = row_count * col_count
    share_count = channels // dev_count
    first_chan = (lax.axis_index("row") * col_count + lax.axis_index("col")) * share_count
    own = lax.all_to_all(video, ("row", "col"), split_axis=4, concat_axis=0, tiled=True)
    own = own.reshape(
        row_count, col_count, clip_count, frame_rows, height_rows, width_cells, share_count
    )
    own = jnp.transpose(own, (2, 6, 0, 3, 1, 4, 5)).reshape(
        clip_count, share_count, frames, height, width_cells
    )
    pieces = sliced_kernels(
        decay_rates,
        frequencies,
        input_vec,
        output_vec,
        lowrank_vec,
        step_scale,
        first_chan,
        share_count,
        lengths,
    )
    time_mat = circulant(pieces[0], frames, True)
    height_mat = circulant(pieces[1], height, False)
    width_mat = circulant(pieces[2], width_cells, False)
    result = jnp.einsum("ctu,bcuhw->bcthw", time_mat, own, precision=full_precision)
    result = jnp.einsum("chg,bctgw->bcthw", height_mat, result, precision=full_precision)
    result = jnp.einsum("cwv,bcthv->bcthw", width_mat, result, precision=full_precision)
    gains = lax.dynamic_slice_in_dim(skip_gain, first_chan, share_count, 0)
    result = jax.nn.gelu(result + gains[None, :, None, None, None] * own, approximate=False)
    result = result.reshape(
        clip_count, share_count, row_count, frame_rows, col_count, height_rows, width_cells
    )
    result = jnp.transpose(result, (2, 4, 0, 3, 5, 6, 1)).reshape(
        dev_count * clip_count, frame_rows, height_rows, width_cells, share_count
    )
    return lax.all_to_all(result, ("row", "col"), split_axis=0, concat_axis=4, tiled=True)


def solution(mesh):
    in_specs = (P(None, "row", "col", None, None), P(), P(), P(), P(), P(), P(), P())
    out_specs = P(None, "row", "col", None, None)
    return jax.shard_map(
        on_device, mesh=mesh, in_specs=in_specs, out_specs=out_specs, check_vma=False
    )
```

profile of v0, /device:TPU:0, one launch (start us, length us, event | category | flops | bytes accessed | tf_op | source)
XLA Modules:
  0.0 1362.8 jit_solution(16412183991252067491)
XLA Ops:
  0.0 30.4 %copy.39 = f32[1,32,8,64,256]{3,2,1,0,4:T(8,128)} copy(f32[1,32,8,64,256]{4,3,2,1,0:T(8,128)} %param.8) | data formatting | bytes 33554432 | tf_op args[0]
  30.4 35.6 %reshape.610 = f32[32,1,131072]{2,1,0:T(1,128)} reshape(f32[256,1,32,8,64]{4,3,2,1,0:T(8,128)} %bitcast.457) | data formatting | bytes 33554432
  66.1 7.5 all-to-all-start
  74.8 1.2 fusion.42
  76.0 1.2 fusion.29
  77.2 1.2 fusion.27
  78.4 1.2 fusion.43
  79.6 1.2 fusion.44
  80.8 1.2 fusion.35
  81.9 1.2 fusion.31
  83.1 1.2 fusion.46
  84.3 1.2 fusion.45
  85.5 1.2 fusion.37
  86.7 1.2 fusion.33
  87.9 1.2 fusion.47
  89.1 1.2 fusion.39
  90.3 1.2 fusion.41
  91.4 1.2 fusion.48
  92.6 1.3 fusion.25
  95.0 54.8 %gather_fusion = f32[16384,8]{1,0:T(8,128)} fusion(f32[8,128]{0,1:T(8,128)S(1)} %copy.37, s32[16384]{0:T(1024)S(1)} %fusion.102), kind=kCustom, calls=%fused_computation | custom fusion | bytes 1114112 | tf_op jit(solution)/shard_map/gather | solution.py:107
  149.8 5.1 copy.38
  157.1 0.7 fusion.67
  157.8 0.7 fusion.54
  158.5 0.7 fusion.68
  159.2 0.7 fusion.92
  160.6 0.7 fusion.91
  162.0 0.7 fusion.93
  164.1 0.7 fusion.95
  164.8 0.7 fusion.94
  166.9 0.7 fusion.96
  167.6 0.7 fusion.88
  168.3 0.7 fusion.90
  169.0 0.7 fusion.97
  171.2 11.0 gather_fusion.1
  183.2 0.7 fusion.69
  184.0 0.7 fusion.60
  185.4 0.7 fusion.71
  186.1 0.7 fusion.70
  186.8 0.7 fusion.62
  188.2 0.7 fusion.72
  188.9 0.7 fusion.64
  189.6 0.7 fusion.66
  190.3 0.7 fusion.73
  191.0 0.7 fusion.50
  192.3 10.8 gather_fusion.2
  203.8 244.8 %all-to-all-done = f32[32,1,131072]{2,1,0:T(1,128)} async-done(((f32[32,1,131072]{2,1,0:T(1,128)}), f32[32,1,131072]{2,1,0:T(1,128)}, u32[]{:S(2)}, u32[]{:S(2)}) %all-to-all-start) | async-done | bytes 16777248 | tf_op jit(solution)/shard_map/all_to_all | solution.py:124
  449.1 48.4 %reduce = f32[32,131072]{1,0:T(8,128)} reduce(f32[32,1,131072]{2,1,0:T(1,128)} %all-to-all-done, f32[]{:T(128)} %broadcast.530), dimensions={1}, to_apply=%all_to_all.24.reduce_sub_computation | reduce | bytes 33554436 | tf_op jit(solution)/shard_map/all_to_all | solution.py:124
  497.5 35.2 %reshape.611 = f32[256,1,32,8,64]{4,3,2,1,0:T(8,128)} reshape(f32[32,131072]{1,0:T(8,128)} %reduce) | data formatting | bytes 33554432
  532.7 28.3 %copy.149 = f32[1,32,8,64,256]{3,4,2,1,0:T(8,128)S(1)} copy(f32[1,32,8,64,256]{3,2,1,0,4:T(8,128)} %bitcast.458) | data formatting | bytes 33554432 | tf_op jit(solution)/shard_map/all_to_all | solution.py:124
  561.0 12.2 copy.41
  573.2 27.6 %copy.42 = f32[1,8,4,32,8,8,64]{6,5,4,3,2,1,0:T(8,128)} copy(f32[1,8,4,32,8,8,64]{6,1,5,3,0,4,2:T(8,128)} %bitcast.460) | data formatting | bytes 33554432 | tf_op jit(solution)/shard_map/transpose | solution.py:128
  600.8 27.4 %copy.53 = f32[8,128,64,64]{1,3,2,0:T(8,128)} copy(f32[8,128,64,64]{3,2,1,0:T(8,128)} %bitcast.455) | data formatting | bytes 33554432 | tf_op jit(solution)/shard_map/reshape.29
  628.2 29.5 %copy.43 = f32[8,128,64,64]{1,2,3,0:T(8,128)} copy(f32[8,128,64,64]{3,2,1,0:T(8,128)} %bitcast.456) | data formatting | bytes 33554432 | tf_op jit(solution)/shard_map/reshape.29
  657.6 18.9 %fusion.16 = f32[8,128,64,64]{1,2,3,0:T(8,128)} fusion(f32[8,128,64,64]{1,2,3,0:T(8,128)} %copy.43, f32[128,128,8]{1,0,2:T(8,128)S(1)} %copy.38, pred[128,128]{1,0:T(8,128)(4,1)S(1)} %subtract_compare_fusion), kind=kOutput, calls=%fused_computation.33 | convolution fusion | flops 6442582016 | bytes 34095104 | tf_op jit(solution)/shard_map/ctu,bcuhw->bcthw/dot_general | solution.py:145
  676.5 21.4 %convolution_bitcast_fusion = f32[8,128,64,64]{1,2,3,0:T(8,128)} fusion(f32[8,128,64,64]{1,2,3,0:T(8,128)} %fusion.16, f32[64,64,8]{1,0,2:T(8,128)S(1)} %copy.47), kind=kOutput, calls=%fused_computation.26 | convolution fusion | flops 3221225472 | bytes 33685504 | tf_op jit(solution)/shard_map/chg,bctgw->bcthw/dot_general | solution.py:146
  697.9 67.0 %fusion.1 = f32[8,128,64,64]{1,3,2,0:T(8,128)} fusion(f32[8,128,64,64]{1,3,2,0:T(8,128)} %copy.53, f32[8,128,64,64]{1,2,3,0:T(8,128)} %convolution_bitcast_fusion, f32[8]{0:T(128)S(1)} %dynamic_slice.75, f32[64,64,8]{1,0,2:T(8,128)S(1)} %copy.51), kind=kOutput, calls=%fused_computation.7 | convolution fusion | flops 3498049536 | bytes 50462752 | tf_op jit(solution)/shard_map/cwv,bcthv->bcthw/dot_general | solution.py:147
  764.9 30.5 %copy.54 = f32[8,128,64,64]{3,2,1,0:T(8,128)} copy(f32[8,128,64,64]{1,3,2,0:T(8,128)} %fusion.1) | data formatting | bytes 33554432 | tf_op jit(solution)/shard_map/mul | solution.py:149
  795.3 32.2 %copy.55 = f32[4,8,1,32,8,64,8]{5,6,4,3,2,1,0:T(8,128)} copy(f32[4,8,1,32,8,64,8]{5,4,1,3,0,6,2:T(8,128)} %bitcast.461) | data formatting | bytes 33554432 | tf_op jit(solution)/shard_map/transpose | solution.py:153
  827.5 35.6 %reshape.612 = f32[32,1,131072]{2,1,0:T(1,128)} reshape(f32[32,32,8,8,64]{4,3,2,1,0:T(8,128)} %bitcast.462) | data formatting | bytes 33554432
  863.1 368.3 %all_to_all.33 = f32[32,1,131072]{2,1,0:T(1,128)} all-to-all(f32[32,1,131072]{2,1,0:T(1,128)} %reshape.612), channel_id=1, replica_groups=mesh['row'=4,'col'=8] {'row','col'}, dimensions={0} | all-to-all | bytes 33554432 | tf_op jit(solution)/shard_map/all_to_all | solution.py:156
  1231.5 48.4 %reduce.1 = f32[32,131072]{1,0:T(8,128)} reduce(f32[32,1,131072]{2,1,0:T(1,128)} %all_to_all.33, f32[]{:T(128)} %broadcast.530), dimensions={1}, to_apply=%all_to_all.27.reduce_sub_computation | reduce | bytes 33554436 | tf_op jit(solution)/shard_map/all_to_all | solution.py:156
  1279.8 34.9 %reshape.613 = f32[32,32,8,8,64]{4,3,2,1,0:T(8,128)} reshape(f32[32,131072]{1,0:T(8,128)} %reduce.1) | data formatting | bytes 33554432
  1314.7 23.2 %copy_bitcast_fusion = f32[1,32,8,64,256]{3,4,2,1,0:T(8,128)} fusion(f32[32,32,8,8,64]{4,3,2,1,0:T(8,128)} %reshape.613), kind=kLoop, calls=%fused_computation.3 | loop fusion | bytes 33554432 | tf_op jit(solution)/shard_map/all_to_all | solution.py:156
  1337.9 24.5 %copy.57 = f32[1,32,8,64,256]{4,3,2,1,0:T(8,128)} copy(f32[1,32,8,64,256]{3,4,2,1,0:T(8,128)} %copy_bitcast_fusion) | data formatting | bytes 33554432 | tf_op jit(solution)/shard_map/all_to_all | solution.py:156
  (94 shorter events, 14.3 us)
Async XLA Ops:
  66.0 7.5 copy-start
  66.0 7.6 copy-start.1
  66.0 7.6 copy-start.2
  66.0 7.8 copy-start.3
  66.0 7.9 copy-start.4
  66.0 8.5 copy-start.5
  66.1 382.5 %all-to-all-start = ((f32[32,1,131072]{2,1,0:T(1,128)}), f32[32,1,131072]{2,1,0:T(1,128)}, u32[]{:S(2)}, u32[]{:S(2)}) async-start(f32[32,1,131072]{2,1,0:T(1,128)} %reshape.610), calls=%async_computation | async-start | bytes 33554432 | tf_op jit(solution)/shard_map/all_to_all | solution.py:124
  158.5 24.3 %copy-start.6 = (f32[256]{0:T(256)S(1)}, f32[256]{0:T(256)}, u32[]{:S(2)}) copy-start(f32[256]{0:T(256)} %param.15) | copy-start | bytes 3076
where the time goes:
time: 1380 us; the launch traced here: 1360 us
  local copies, waits for them, and re-layouts  493 us (36%)
  blocking collectives  368 us (27%)
  waiting for transfers between devices  245 us (18%)
  matrix products  151 us (11%)
  other arithmetic  97.8 us (7%)
    all_to_all x1, blocking collectives, on_device(): lax.all_to_all(result, ('row', 'col'), split_axis=0, concat_axis=4, tiled...  368 us
    all_to_all x1, waiting for transfers between devices, on_device(): lax.all_to_all(video, ('row', 'col'), split_axis=4, concat_axis=0, tiled=...  245 us
    unnamed x25, local copies, waits for them, and re-layouts  172 us
    dot_general x1, matrix products, on_device(): jnp.einsum('cwv,bcthv->bcthw', width_mat, result, precision=full_precision)  67 us
    gather x2, local copies, waits for them, and re-layouts, circulant(): table = kernel.T[:, jnp.clip(offset, 0, length - 1)]  60 us
    another operation x3, local copies, waits for them, and re-layouts  56.9 us
    all_to_all x1, other arithmetic, on_device(): lax.all_to_all(result, ('row', 'col'), split_axis=0, concat_axis=4, tiled...  48.4 us
    all_to_all x1, other arithmetic, on_device(): lax.all_to_all(video, ('row', 'col'), split_axis=4, concat_axis=0, tiled=...  48.4 us
  transfers between devices with their start and end apart: 1, of which 1 were waited for; matrix products, arithmetic and copies ran while one was open for 10% of the time, Pallas kernels for 0%

commit v1 on v0

v1 whole, which is shorter than its diff:
```python
import functools
import math

import jax
import jax.numpy as jnp
from jax import lax
from jax.experimental import pallas as pl
from jax.experimental.pallas import tpu as pltpu
from jax.sharding import PartitionSpec as P

full_precision = lax.Precision.HIGHEST
LANES = 128
SUBLANES = 8
CHUNKS = 2


def complex_mul(left_re, left_im, right_re, right_im):
    return (left_re * right_re - left_im * right_im, left_re * right_im + left_im * right_re)


def complex_div(left_re, left_im, right_re, right_im):
    magnitude = right_re * right_re + right_im * right_im
    return (
        (left_re * right_re + left_im * right_im) / magnitude,
        (left_im * right_re - left_re * right_im) / magnitude,
    )


def cauchy_sum(num_re, num_im, inv_re, inv_im):
    num_re, num_im = num_re[:, None, :], num_im[:, None, :]
    return (
        jnp.sum(num_re * inv_re - num_im * inv_im, -1),
        jnp.sum(num_re * inv_im + num_im * inv_re, -1),
    )


def axis_rows(decay, oscill, input_part, output_part, lowrank_part, scales, length, lags):
    step_size = scales / length
    two_over = (2.0 / step_size)[:, None, None]
    index = jnp.arange(length, dtype=jnp.int32)
    angles = 2.0 * math.pi / length * index.astype(jnp.float32)
    cosine = jnp.cos(angles)
    sine_vals = jnp.sin(angles)
    minus_cos = (1.0 - cosine)[None, :, None]
    plus_cos = (1.0 + cosine)[None, :, None]
    sine_col = sine_vals[None, :, None]
    den_re = two_over * minus_cos + decay[:, None, :] * plus_cos - oscill[:, None, :] * sine_col
    den_im = two_over * sine_col - decay[:, None, :] * sine_col - oscill[:, None, :] * plus_cos
    magnitude = den_re * den_re + den_im * den_im
    inv_re = den_re / magnitude
    inv_im = -den_im / magnitude
    prod_cb = complex_mul(output_part[0], output_part[1], input_part[0], input_part[1])
    prod_cp = complex_mul(output_part[0], output_part[1], lowrank_part[0], lowrank_part[1])
    prod_pb = complex_mul(lowrank_part[0], -lowrank_part[1], input_part[0], input_part[1])
    prod_pp = lowrank_part[0] * lowrank_part[0] + lowrank_part[1] * lowrank_part[1]
    cauchy_cb = cauchy_sum(prod_cb[0], prod_cb[1], inv_re, inv_im)
    cauchy_cp = cauchy_sum(prod_cp[0], prod_cp[1], inv_re, inv_im)
    cauchy_pb = cauchy_sum(prod_pb[0], prod_pb[1], inv_re, inv_im)
    cauchy_pp = cauchy_sum(prod_pp, jnp.zeros_like(prod_pp), inv_re, inv_im)
    shift_re = (1.0 + cosine)[None, :]
    shift_im = (-sine_vals)[None, :]
    cross_re, cross_im = complex_mul(cauchy_cp[0], cauchy_cp[1], cauchy_pb[0], cauchy_pb[1])
    cross_re, cross_im = complex_mul(shift_re, shift_im, cross_re, cross_im)
    lower_re, lower_im = complex_mul(shift_re, shift_im, cauchy_pp[0], cauchy_pp[1])
    quot_re, quot_im = complex_div(cross_re, cross_im, 1.0 + lower_re, lower_im)
    gen_re = 2.0 * (cauchy_cb[0] - quot_re)
    gen_im = 2.0 * (cauchy_cb[1] - quot_im)
    table = index[:, None] * (lags % length)[None, :] % length
    table = 2.0 * math.pi / length * table.astype(jnp.float32)
    rows = jnp.dot(gen_re, jnp.cos(table), precision=full_precision) - jnp.dot(
        gen_im, jnp.sin(table), precision=full_precision
    )
    return rows / length


def pack_kernel(frames, pack, src_ref, dst_ref):
    flat = dst_ref.reshape(LANES * frames, LANES)

    @pl.loop(0, frames, unroll=2)
    def _(step):
        tile = src_ref[step].reshape(LANES, LANES)
        flat[pl.ds(step, LANES, stride=frames), :] = tile.T


def pack_chunk(video, chunk, pack):
    frames, height, width, _ = video.shape
    pairs = height // pack
    return pl.pallas_call(
        functools.partial(pack_kernel, frames, pack),
        grid=(pairs,),
        in_specs=[pl.BlockSpec((frames, pack, width, LANES), lambda i: (0, i, 0, chunk))],
        out_specs=pl.BlockSpec((LANES, 1, frames, LANES), lambda i: (0, i, 0, 0)),
        out_shape=jax.ShapeDtypeStruct((LANES, pairs, frames, LANES), jnp.float32),
        cost_estimate=pl.CostEstimate(
            flops=0, transcendentals=0, bytes_accessed=8 * frames * height * width * LANES
        ),
        name="pack",
    )(video)


def unpack_kernel(frames, pack, src_ref, *refs):
    dst_ref = refs[-1]
    flat = src_ref.reshape(LANES * frames, LANES)
    width = LANES // pack

    @pl.loop(0, frames, unroll=2)
    def _(step):
        tile = flat[pl.ds(step, LANES, stride=frames), :]
        dst_ref[step] = tile.T.reshape(pack, width, LANES)


def unpack_chunk(packed, chunk, pack, shape, into):
    frames, height, width, _ = shape
    pairs = height // pack
    in_specs = [pl.BlockSpec((LANES, 1, frames, LANES), lambda i: (0, i, 0, 0))]
    operands = [packed]
    aliases = {}
    if into is not None:
        in_specs.append(pl.BlockSpec(memory_space=pl.ANY))
        operands.append(into)
        aliases = {1: 0}
    return pl.pallas_call(
        functools.partial(unpack_kernel, frames, pack),
        grid=(pairs,),
        in_specs=in_specs,
        out_specs=pl.BlockSpec((frames, pack, width, LANES), lambda i: (0, i, 0, chunk)),
        out_shape=jax.ShapeDtypeStruct(shape, jnp.float32),
        input_output_aliases=aliases,
        cost_estimate=pl.CostEstimate(
            flops=0, transcendentals=0, bytes_accessed=8 * frames * height * width * LANES
        ),
        name="unpack",
    )(*operands)


def split(value):
    high = value.astype(jnp.bfloat16)
    low = (value - high.astype(jnp.float32)).astype(jnp.bfloat16)
    return high, low


def shifted_rows(row, count):
    return pltpu.roll(jnp.broadcast_to(row, (count, LANES)), 0, 1, stride=1, stride_axis=0)


def dot(left, right):
    return jnp.dot(left, right, preferred_element_type=jnp.float32)


def left_stack(matrix):
    high, low = split(matrix)
    return jnp.concatenate(
        [
            jnp.concatenate([high, high], 1),
            jnp.concatenate([low, jnp.zeros_like(low)], 1),
        ],
        0,
    )


def conv_kernel(dims, taps_ref, src_ref, dst_ref, work):
    row_count, col_count, pairs, frame_rows, pack = dims
    frames = row_count * frame_rows
    quads = col_count * pairs
    width = LANES // pack
    taps = taps_ref[0]

    time_i = lax.broadcasted_iota(jnp.int32, (frames, frames), 0)
    time_j = lax.broadcasted_iota(jnp.int32, (frames, frames), 1)
    time_mat = jnp.where(time_i >= time_j, shifted_rows(taps[0:1], frames)[:, :frames], 0.0)
    time_stack = left_stack(time_mat)

    cell_i = lax.broadcasted_iota(jnp.int32, (LANES, LANES), 0)
    cell_j = lax.broadcasted_iota(jnp.int32, (LANES, LANES), 1)
    width_mat = jnp.where(cell_i // width == cell_j // width, shifted_rows(taps[1:2], LANES), 0.0)
    width_high, width_low = split(width_mat)
    width_stack = jnp.concatenate(
        [
            jnp.concatenate([width_high, width_low], 1),
            jnp.concatenate([width_high, jnp.zeros_like(width_low)], 1),
        ],
        0,
    )

    def load(quad):
        col = quad // pairs
        first = pl.multiple_of(quad % pairs * frame_rows, frame_rows)
        return jnp.concatenate(
            [
                src_ref[row, col, 0, pl.ds(first, frame_rows), :]
                for row in range(row_count)
            ],
            0,
        )

    @pl.loop(0, quads // 2)
    def _(step):
        both = jnp.concatenate([load(2 * step), load(2 * step + 1)], 1)
        high, low = split(both)
        conv = dot(time_stack, jnp.concatenate([high, low], 0))
        conv = conv[:frames] + conv[frames:]
        conv = jnp.concatenate([conv[:, :LANES], conv[:, LANES:]], 0)
        high, low = split(conv)
        conv = dot(jnp.concatenate([high, low], 1), width_stack)
        conv = conv[:, :LANES] + conv[:, LANES:]
        work[pl.ds(pl.multiple_of(2 * frames * step, 2 * frames), 2 * frames), :] = conv

    height_stack = jnp.concatenate(
        [left_stack(shifted_rows(taps[2 + e : 3 + e], quads)[:, :quads]) for e in range(3)], 0
    )
    group = 4
    lane = lax.broadcasted_iota(jnp.int32, (quads, group * LANES), 1) % LANES

    @pl.loop(0, frames // group)
    def _(step):
        tiles = [
            work[pl.ds(group * step + e, quads, stride=frames), :] for e in range(group)
        ]
        high, low = split(jnp.concatenate(tiles, 1))
        conv = dot(height_stack, jnp.concatenate([high, low], 0))
        same = conv[:quads] + conv[quads : 2 * quads]
        upper = conv[2 * quads : 3 * quads] + conv[3 * quads : 4 * quads]
        lower = conv[4 * quads : 5 * quads] + conv[5 * quads :]
        cross = jnp.where(lane < width, upper, lower)
        for e in range(group):
            cols = slice(e * LANES, (e + 1) * LANES)
            work[pl.ds(group * step + e, quads, stride=frames), :] = same[:, cols] + pltpu.roll(
                cross[:, cols], width, 1
            )

    gain = taps[5:6]

    @pl.loop(0, quads)
    def _(quad):
        col = quad // pairs
        first = pl.multiple_of(quad % pairs * frame_rows, frame_rows)
        for row in range(row_count):
            start = pl.multiple_of(quad * frames + row * frame_rows, frame_rows)
            value = work[pl.ds(start, frame_rows), :]
            value = value + gain * src_ref[row, col, 0, pl.ds(first, frame_rows), :]
            value = 0.5 * value * (1.0 + lax.erf(value * math.sqrt(0.5)))
            dst_ref[row, col, 0, pl.ds(first, frame_rows), :] = value


def conv_chunk(packed, taps, row_count, col_count, pairs, frame_rows, pack):
    share = packed.shape[2]
    rows = packed.shape[3]
    frames = row_count * frame_rows
    quads = col_count * pairs
    block = pl.BlockSpec((row_count, col_count, 1, rows, LANES), lambda i: (0, 0, i, 0, 0))
    cells = frames * quads * LANES
    return pl.pallas_call(
        functools.partial(conv_kernel, (row_count, col_count, pairs, frame_rows, pack)),
        grid=(share,),
        in_specs=[pl.BlockSpec((1, SUBLANES, LANES), lambda i: (i, 0, 0)), block],
        out_specs=block,
        out_shape=jax.ShapeDtypeStruct(packed.shape, jnp.float32),
        scratch_shapes=[pltpu.VMEM((quads * frames, LANES), jnp.float32)],
        cost_estimate=pl.CostEstimate(
            flops=share * cells * 2000, transcendentals=share * cells, bytes_accessed=8 * share * cells
        ),
        name="conv",
    )(taps, packed)


def on_device(
    video, decay_rates, frequencies, input_vec, output_vec, lowrank_vec, step_scale, skip_gain
):
    clip_count, frame_rows, height_rows, width_cells, channels = video.shape
    row_count = lax.axis_size("row")
    col_count = lax.axis_size("col")
    frames = frame_rows * row_count
    height = height_rows * col_count
    dev_count = row_count * col_count
    pack = LANES // width_cells
    pairs = height_rows // pack
    chunk_width = channels // CHUNKS
    share = chunk_width // dev_count
    assert clip_count == 1 and pack == 2 and chunk_width == LANES and frames == LANES
    me = lax.axis_index("row") * col_count + lax.axis_index("col")
    shape = video.shape[1:]
    video = video.reshape(shape)

    def own(array, dim):
        split_shape = array.shape[:dim] + (CHUNKS, chunk_width) + array.shape[dim + 1 :]
        part = lax.dynamic_slice_in_dim(array.reshape(split_shape), me * share, share, dim + 1)
        return part.reshape(array.shape[:dim] + (CHUNKS * share,) + array.shape[dim + 1 :])

    def everyone(first):
        return [
            lax.all_to_all(e, ("row", "col"), split_axis=0, concat_axis=0, tiled=True)
            for e in first
        ]

    packed = [pack_chunk(video, chunk, pack) for chunk in range(CHUNKS)]
    packed = everyone(packed)

    decay_rates, frequencies = own(decay_rates, 1), own(frequencies, 1)
    input_vec, output_vec, lowrank_vec = own(input_vec, 2), own(output_vec, 2), own(lowrank_vec, 2)
    step_scale, gains = own(step_scale, 1), own(skip_gain, 0)
    lane = jnp.arange(LANES, dtype=jnp.int32)
    lags = (
        -lane,
        jnp.concatenate([-pack * lane, 1 - pack * lane, -1 - pack * lane]),
        lane,
    )
    time_rows, height_rows_taps, width_rows = (
        axis_rows(
            decay_rates[axis],
            frequencies[axis],
            input_vec[axis],
            output_vec[axis],
            lowrank_vec[axis],
            step_scale[axis],
            length,
            lags[axis],
        )
        for axis, length in enumerate((frames, height, width_cells))
    )
    own_count = CHUNKS * share
    taps = jnp.concatenate(
        [
            time_rows[:, None],
            width_rows[:, None],
            height_rows_taps.reshape(own_count, 3, LANES),
            jnp.broadcast_to(gains[:, None, None], (own_count, SUBLANES - 5, LANES)),
        ],
        1,
    ).reshape(CHUNKS, share, SUBLANES, LANES)

    outs = []
    for chunk in range(CHUNKS):
        block = packed[chunk].reshape(row_count, col_count, share, pairs * frame_rows, LANES)
        block = conv_chunk(block, taps[chunk], row_count, col_count, pairs, frame_rows, pack)
        outs.append(block.reshape(LANES, pairs, frame_rows, LANES))
    outs = everyone(outs)
    result = None
    for chunk in range(CHUNKS):
        result = unpack_chunk(outs[chunk], chunk, pack, shape, result)
    return result.reshape((clip_count,) + shape)


def solution(mesh):
    in_specs = (P(None, "row", "col", None, None), P(), P(), P(), P(), P(), P(), P())
    out_specs = P(None, "row", "col", None, None)
    return jax.shard_map(
        on_device, mesh=mesh, in_specs=in_specs, out_specs=out_specs, check_vma=False
    )
```

time: 1380 us -> 803 us (0.58); the launches traced: 1360 us -> 802 us
  local copies, waits for them, and re-layouts: 493 us -> 2.84 us
  blocking collectives: 368 us -> 0 us
  waiting for transfers between devices: 245 us -> 575 us
  Pallas kernels: 0 us -> 200 us
  matrix products: 151 us -> 2.5 us
  other arithmetic: 97.8 us -> 3.64 us
    all_to_all x1 -> x0, blocking collectives: 368 us -> none  [on_device(): lax.all_to_all(result, ('row', 'col'), split_axis=0, concat_axis=4, tiled...]
    all_to_all x1 -> x4, waiting for transfers between devices: 245 us -> 575 us  [everyone(): lax.all_to_all(e, ('row', 'col'), split_axis=0, concat_axis=0, tiled=True)]
    pallas_call x0 -> x6, Pallas kernels: none -> 200 us  [the longest x2 149 us: conv_chunk(): pl.pallas_call(functools.partial(conv_kernel, (row_count, col_count, pair...]
    unnamed x25 -> x16, local copies, waits for them, and re-layouts: 172 us -> 0.04 us
    dot_general x57 -> x6, matrix products: 151 us -> 2.5 us  [the longest x3 1.28 us: axis_rows(): jnp.dot(gen_im, jnp.sin(table), precision=full_precision)]
    all_to_all x2 -> x0, other arithmetic: 96.7 us -> none  [the longest x1 48.4 us: on_device(): lax.all_to_all(result, ('row', 'col'), split_axis=0, concat_axis=4, tiled...]
    all_to_all x5 -> x0, local copies, waits for them, and re-layouts: 88.7 us -> none  [the longest x2 47.7 us: on_device(): lax.all_to_all(result, ('row', 'col'), split_axis=0, concat_axis=4, tiled...]
    gather x6 -> x0, local copies, waits for them, and re-layouts: 82.9 us -> none  [the longest x2 60 us: circulant(): table = kernel.T[:, jnp.clip(offset, 0, length - 1)]]
  transfers between devices with their start and end apart: 1 -> 4, of which waited for: 1 -> 4; matrix products, arithmetic and copies ran while one was open for 10% -> 1% of each run, Pallas kernels for 0% -> 22%
where the time goes in v1:
time: 803 us; the launch traced here: 802 us
  waiting for transfers between devices  575 us (72%)
  Pallas kernels  200 us (25%)
  starting transfers between devices  18.5 us (2%)
    all_to_all x4, waiting for transfers between devices, everyone(): lax.all_to_all(e, ('row', 'col'), split_axis=0, concat_axis=0, tiled=True)  575 us
    pallas_call x2, Pallas kernels, conv_chunk(): pl.pallas_call(functools.partial(conv_kernel, (row_count, col_count, pair...  149 us
    pallas_call x2, Pallas kernels, pack_chunk(): pl.pallas_call(functools.partial(pack_kernel, frames, pack), grid=(pairs,...  26.1 us
    pallas_call x2, Pallas kernels, unpack_chunk(): pl.pallas_call(functools.partial(unpack_kernel, frames, pack), grid=(pair...  24.1 us
    all_to_all x4, starting transfers between devices, everyone(): lax.all_to_all(e, ('row', 'col'), split_axis=0, concat_axis=0, tiled=True)  18.5 us
  transfers between devices with their start and end apart: 4, of which 4 were waited for; matrix products, arithmetic and copies ran while one was open for 1% of the time, Pallas kernels for 22%

profile of v1, /device:TPU:0, one launch (start us, length us, event | category | flops | bytes accessed | tf_op | source)
XLA Modules:
  0.0 802.3 jit_solution(3527982178079266724)
XLA Ops:
  0.0 0.0 copy-start
  0.0 13.1 %pack.3 = f32[128,4,32,128]{3,2,1,0:T(8,128)} custom-call(f32[32,8,64,256]{3,2,1,0:T(8,128)} %bitcast.41), custom_call_target="tpu_custom_call" | custom-call | bytes 16777216 | tf_op jit(solution)/shard_map/pack/pallas_call | solution.py:88
  13.1 7.5 all-to-all-start.2
  20.5 13.0 %pack.2 = f32[128,4,32,128]{3,2,1,0:T(8,128)} custom-call(f32[32,8,64,256]{3,2,1,0:T(8,128)} %bitcast.42), custom_call_target="tpu_custom_call" | custom-call | bytes 16777216 | tf_op jit(solution)/shard_map/pack/pallas_call | solution.py:88
  33.6 0.0 copy-start.7
  33.6 0.0 copy-start.5
  33.6 0.0 copy-start.6
  33.6 0.0 copy-start.2
  33.6 0.0 copy-start.3
  33.6 0.0 copy-start.4
  33.6 176.7 %all-to-all-done.2 = f32[128,4,32,128]{3,2,1,0:T(8,128)} async-done(((f32[128,4,32,128]{3,2,1,0:T(8,128)}), f32[128,4,32,128]{3,2,1,0:T(8,128)}, u32[]{:S(2)}, u32[]{:S(2)}) %all-to-all-start.2) | async-done | bytes 8388640 | tf_op jit(solution)/shard_map/all_to_all | solution.py:291
  210.3 3.7 all-to-all-start
  214.0 0.0 copy-done
  214.0 0.1 constant_dynamic-slice_fusion.21
  214.1 0.1 broadcast_in_dim.10
  214.2 0.0 copy-done.7
  214.2 0.1 fusion.94
  214.3 0.1 div.95
  214.4 0.1 div.104
  214.5 0.6 div.113
  215.0 0.0 copy-done.5
  215.0 0.2 copy.51
  215.2 0.0 copy-done.6
  215.2 0.2 copy.52
  215.4 0.0 copy-done.2
  215.4 0.3 copy.50
  215.7 0.0 copy-done.3
  215.7 0.3 copy.49
  215.9 0.0 copy-done.4
  216.0 0.3 copy.53
  216.5 0.7 broadcast_multiply_fusion.3
  217.1 0.8 add_reduce_fusion
  218.0 0.5 fusion.11
  218.5 0.6 fusion.1
  219.2 0.1 broadcast_multiply_fusion.5
  219.3 0.8 add_reduce_fusion.8
  220.2 0.8 add_reduce_fusion.4
  221.0 0.3 fusion.31
  221.3 0.4 fusion.20
  221.7 0.4 fusion.3
  222.2 0.3 fusion.2
  222.4 0.1 broadcast_in_dim.11
  222.6 0.6 fusion.138
  223.2 74.6 %conv.3 = f32[4,8,4,128,128]{4,3,2,1,0:T(8,128)} custom-call(f32[4,8,128]{2,1,0:T(8,128)} %get-tuple-element.71.taps_ref, f32[4,8,4,128,128]{4,3,2,1,0:T(8,128)} %bitcast.36.src_ref), custom_call_target="tpu_custom_call" | custom-call | flops 4194304000 | bytes 16777216 | tf_op jit(solution)/shard_map/conv/pallas_call | solution.py:252
  297.8 105.8 %all-to-all-done = f32[128,4,32,128]{3,2,1,0:T(8,128)} async-done(((f32[128,4,32,128]{3,2,1,0:T(8,128)}), f32[128,4,32,128]{3,2,1,0:T(8,128)}, u32[]{:S(2)}, u32[]{:S(2)}) %all-to-all-start) | async-done | bytes 8388640 | tf_op jit(solution)/shard_map/all_to_all | solution.py:291
  403.6 3.7 all-to-all-start.3
  407.3 74.8 %conv.2 = f32[4,8,4,128,128]{4,3,2,1,0:T(8,128)} custom-call(f32[4,8,128]{2,1,0:T(8,128)} %get-tuple-element.72.taps_ref, f32[4,8,4,128,128]{4,3,2,1,0:T(8,128)} %bitcast.34.src_ref), custom_call_target="tpu_custom_call" | custom-call | flops 4194304000 | bytes 16777216 | tf_op jit(solution)/shard_map/conv/pallas_call | solution.py:252
  482.1 114.9 %all-to-all-done.3.src_ref = f32[128,4,32,128]{3,2,1,0:T(8,128)} async-done(((f32[128,4,32,128]{3,2,1,0:T(8,128)}), f32[128,4,32,128]{3,2,1,0:T(8,128)}, u32[]{:S(2)}, u32[]{:S(2)}) %all-to-all-start.3) | async-done | bytes 8388640 | tf_op jit(solution)/shard_map/all_to_all | solution.py:291
  597.0 3.7 all-to-all-start.1
  600.6 12.1 %unpack.2.refs_0_ = f32[32,8,64,256]{3,2,1,0:T(8,128)} custom-call(f32[128,4,32,128]{3,2,1,0:T(8,128)} %all-to-all-done.3.src_ref), custom_call_target="tpu_custom_call" | custom-call | bytes 16777216 | tf_op jit(solution)/shard_map/unpack/pallas_call | solution.py:122
  612.7 177.6 %all-to-all-done.1.src_ref = f32[128,4,32,128]{3,2,1,0:T(8,128)} async-done(((f32[128,4,32,128]{3,2,1,0:T(8,128)}), f32[128,4,32,128]{3,2,1,0:T(8,128)}, u32[]{:S(2)}, u32[]{:S(2)}) %all-to-all-start.1) | async-done | bytes 8388640 | tf_op jit(solution)/shard_map/all_to_all | solution.py:291
  790.3 0.0 copy-start.1
  790.3 12.1 %unpack.3 = f32[32,8,64,256]{3,2,1,0:T(8,128)} custom-call(f32[128,4,32,128]{3,2,1,0:T(8,128)} %all-to-all-done.1.src_ref, f32[32,8,64,256]{3,2,1,0:T(8,128)} %unpack.2.refs_0_), custom_call_target="tpu_custom_call", output_to_operand_aliasing={{}: (1, {})} | custom-call | bytes 16777216 | tf_op jit(solution)/shard_map/unpack/pallas_call | solution.py:122
  802.3 0.0 copy-done.1
  (20 shorter events, 0.4 us)
Async XLA Ops:
  0.0 214.0 %copy-start = (f32[256]{0:T(256)S(1)}, f32[256]{0:T(256)}, u32[]{:S(2)}) copy-start(f32[256]{0:T(256)} %param.15) | copy-start | bytes 3076
  13.1 197.3 %all-to-all-start.2 = ((f32[128,4,32,128]{3,2,1,0:T(8,128)}), f32[128,4,32,128]{3,2,1,0:T(8,128)}, u32[]{:S(2)}, u32[]{:S(2)}) async-start(f32[128,4,32,128]{3,2,1,0:T(8,128)} %pack.3), calls=%async_computation.2 | async-start | bytes 16777216 | tf_op jit(solution)/shard_map/all_to_all | solution.py:291
  33.6 180.6 %copy-start.7 = (f32[3,256]{1,0:T(4,128)S(1)}, f32[3,256]{1,0:T(4,128)}, u32[]{:S(2)}) copy-start(f32[3,256]{1,0:T(4,128)} %param.14) | copy-start | bytes 9220
  33.6 181.5 %copy-start.5 = (f32[3,256,64]{1,2,0:T(8,128)S(1)}, f32[3,256,64]{1,2,0:T(8,128)}, u32[]{:S(2)}) copy-start(f32[3,256,64]{1,2,0:T(8,128)} %param.9) | copy-start | bytes 589828
  33.6 181.6 %copy-start.6 = (f32[3,256,64]{1,2,0:T(8,128)S(1)}, f32[3,256,64]{1,2,0:T(8,128)}, u32[]{:S(2)}) copy-start(f32[3,256,64]{1,2,0:T(8,128)} %param.10) | copy-start | bytes 589828
  33.6 181.8 %copy-start.2 = (f32[3,2,256,64]{2,3,1,0:T(8,128)S(1)}, f32[3,2,256,64]{2,3,1,0:T(8,128)}, u32[]{:S(2)}) copy-start(f32[3,2,256,64]{2,3,1,0:T(8,128)} %param.11) | copy-start | bytes 1179652
  33.6 182.1 %copy-start.3 = (f32[3,2,256,64]{2,3,1,0:T(8,128)S(1)}, f32[3,2,256,64]{2,3,1,0:T(8,128)}, u32[]{:S(2)}) copy-start(f32[3,2,256,64]{2,3,1,0:T(8,128)} %param.12) | copy-start | bytes 1179652
  33.6 182.4 %copy-start.4 = (f32[3,2,256,64]{2,3,1,0:T(8,128)S(1)}, f32[3,2,256,64]{2,3,1,0:T(8,128)}, u32[]{:S(2)}) copy-start(f32[3,2,256,64]{2,3,1,0:T(8,128)} %param.13) | copy-start | bytes 1179652
  210.3 193.3 %all-to-all-start = ((f32[128,4,32,128]{3,2,1,0:T(8,128)}), f32[128,4,32,128]{3,2,1,0:T(8,128)}, u32[]{:S(2)}, u32[]{:S(2)}) async-start(f32[128,4,32,128]{3,2,1,0:T(8,128)} %pack.2), calls=%async_computation | async-start | bytes 16777216 | tf_op jit(solution)/shard_map/all_to_all | solution.py:291
  403.6 193.3 %all-to-all-start.3 = ((f32[128,4,32,128]{3,2,1,0:T(8,128)}), f32[128,4,32,128]{3,2,1,0:T(8,128)}, u32[]{:S(2)}, u32[]{:S(2)}) async-start(f32[128,4,32,128]{3,2,1,0:T(8,128)} %bitcast.43), calls=%async_computation.3 | async-start | bytes 16777216 | tf_op jit(solution)/shard_map/all_to_all | solution.py:291
  597.0 193.3 %all-to-all-start.1 = ((f32[128,4,32,128]{3,2,1,0:T(8,128)}), f32[128,4,32,128]{3,2,1,0:T(8,128)}, u32[]{:S(2)}, u32[]{:S(2)}) async-start(f32[128,4,32,128]{3,2,1,0:T(8,128)} %bitcast.44), calls=%async_computation.1 | async-start | bytes 16777216 | tf_op jit(solution)/shard_map/all_to_all | solution.py:291
  790.3 12.1 %copy-start.1 = (f32[256]{0:T(256)S(1)}, f32[256]{0:T(256)}, u32[]{:S(2)}) copy-start(f32[256]{0:T(256)} %param.15) | copy-start | bytes 3076
